TPU v7x, 32 devices: a whole 2x2x4 slice. The times are simulated.
32 devices in a mesh: dp: 32 (over z, y, x, core).
Axes of the slice: x: 2, y: 2, z: 4, core: 2. Of those that a mesh axis runs over, the one named last changes fastest.
Arguments:
- events: bfloat16 [32768, 512], P('dp'), may hold values from -6 to 6
- home_slot: int32 [32768], P('dp'), may hold values from 0 to 1024, as said below
- dest_slot: int32 [32768], P('dp'), may hold values from 0 to 1024, as said below
- seq_lens: int32 [64], P('dp'), may hold values from 0 to 1024, as said below
- weights: bfloat16 [512, 2560], replicated, may hold values from -0.25 to 0.25
- out_grad: bfloat16 [32768, 512], P('dp'), may hold values from -6 to 6
- momentum_in: float32 [512, 2048], P('dp'), may hold values from -3 to 3
- momentum_out: float32 [512, 512], P('dp'), may hold values from -3 to 3
Outputs:
- event_grad: bfloat16 [32768, 512], P('dp')
- new_momentum_in: float32 [512, 2048], P('dp')
- new_momentum_out: float32 [512, 512], P('dp')
Inputs may be any that keep to these rules, and one draw needn't show every extreme that they name: `seq_lens`: each device's 2 entries are the lengths of the sequences placed on it, in order, then zeros; the sequences' blocks, ceil(length / 512) each, add up to at most 2. `dest_slot`: for each row of a device's blocks: 1024 if the row lies in no sequence, else s * 32 + k, where s is the device that holds the row's event at home and k its slot among the rows that s sends to this device; no value below 1024 repeats on a device. `home_slot`: for each home row: 1024 if no sequence uses it, else t * 32 + k, where t is the device that takes the row and k its slot as in dest_slot; no value below 1024 repeats on a device, and the two arrays name the same rows. A device sends at most 32 rows to one device, and in every draw some device receives 32 rows from every device.
All inputs are finite; a program needn't handle non-finite values.
Results may differ from a plain program's by a relative error of at most 0.0085.
Values may be sent and summed in bfloat16 or wider, within the bound.
A program may use at most 128 MiB of HBM per device.

v0:
```python
import functools

import jax
import jax.numpy as jnp
from jax import lax
from jax.experimental import pallas as pl
from jax.experimental.pallas import tpu as pltpu
from jax.sharding import PartitionSpec as P

HEADS = 8
BLK = 512
QB = 256
NORM_EPS = 1e-05
DECAY = 0.9
MESH = pl.DeviceIdType.MESH
F32 = jnp.float32
BF16 = jnp.bfloat16
VMEM_LIMIT = 66 * 1000 * 1000


def dot_nn(a, b):
    return lax.dot_general(a, b, (((1,), (0,)), ((), ())), preferred_element_type=F32)


def dot_nt(a, b):
    return lax.dot_general(a, b, (((1,), (1,)), ((), ())), preferred_element_type=F32)


def dot_tn(a, b):
    return lax.dot_general(a, b, (((0,), (0,)), ((), ())), preferred_element_type=F32)


def chain_bits(bit_count, second):
    order = list(range(bit_count))
    if second and bit_count > 2:
        order[1], order[2] = order[2], order[1]
    return order


def enter_all(n, me):
    barrier = pltpu.get_barrier_semaphore()

    def greet(i, carry):
        pl.semaphore_signal(barrier, inc=1, device_id=((me + i) % n,), device_id_type=MESH)
        return carry

    lax.fori_loop(1, n, greet, 0)
    return barrier


def exchange(n, me, src, dst, ssem, rsem, i):
    peer = (me + i) % n
    return pltpu.make_async_remote_copy(
        src_ref=src.at[peer],
        dst_ref=dst.at[me],
        send_sem=ssem.at[i],
        recv_sem=rsem.at[i],
        device_id=(peer,),
        device_id_type=MESH,
    )


def start_exchange(n, me, src, dst, ssem, rsem):
    def go(i, carry):
        exchange(n, me, src, dst, ssem, rsem, i).start()
        return carry

    lax.fori_loop(n // 2, n, go, 0)
    lax.fori_loop(1, n // 2, go, 0)


def finish_exchange(n, me, src, dst, ssem, rsem):
    def end(i, carry):
        exchange(n, me, src, dst, ssem, rsem, i).wait()
        return carry

    lax.fori_loop(1, n, end, 0)


def gather_matrix(slots_ref, out_ref):
    rows = out_ref.shape[0]
    wide = jnp.broadcast_to(slots_ref[...].astype(F32), (128, rows))
    column = jnp.transpose(wide)
    lane = lax.broadcasted_iota(jnp.int32, (rows, 128), 1).astype(F32)
    for j in range(rows // 128):
        out_ref[:, j * 128 : (j + 1) * 128] = jnp.where(
            column == lane + float(j * 128), 1.0, 0.0
        ).astype(BF16)


def scatter_chunk(slots_ref, start, size):
    rows = slots_ref.shape[1]
    place = lax.broadcasted_iota(jnp.int32, (size, rows), 0) + start
    return jnp.where(place == slots_ref[...], 1.0, 0.0).astype(BF16)


def owner_of(place, lens_ref, none):
    owner = jnp.full(place.shape, none, jnp.int32)
    start = 0
    for j in range(lens_ref.shape[0]):
        length = lens_ref[j]
        inside = (place >= start) & (place < start + length)
        owner = jnp.where(inside, j, owner)
        start = start + (length + BLK - 1) // BLK * BLK
    return owner


def order_matrix(height, width, n, per, bits, fold, turn):
    shape = (height, width)
    tall = per * fold
    place = lax.broadcasted_iota(jnp.int32, shape, 0)
    column = lax.broadcasted_iota(jnp.int32, shape, 1)
    slot = place // tall
    rest = place % tall
    device = jnp.zeros(shape, jnp.int32)
    for rank, bit in enumerate(bits):
        weight = n >> (rank + 1)
        device = device + ((slot // weight) % 2) * (1 << bit)
    hit = (column == device * per + rest % per) & (rest // per == turn)
    return jnp.where(hit, 1.0, 0.0).astype(BF16)


def step_kernel(
    n, lens_ref, home_ref, dest_ref, ev_ref, w_hbm, og_hbm,
    ret_ref, f0_ref, f1_ref, f2_ref, f3_ref,
    w_ref, og_ref, outbox, inbox, inbox2, pick, tok_ref, dmix,
    slope, gate, qs, ks, vs, att, hgrad, mask, mask_t, mixed, dout, acc_k, acc_v, tp,
    lsem, ssem, rsem, ssem2, rsem2, hs, hr, *bufs,
):
    me = lax.axis_index("dp")
    rows, width = ev_ref.shape
    cap = rows // n
    per = width // n
    fold = max(1, 16 // per)
    nq = rows // QB
    bits = n.bit_length() - 1
    group = QB // cap
    barrier = enter_all(n, me)
    load_w = pltpu.make_async_copy(w_hbm, w_ref, lsem.at[0])
    load_og = pltpu.make_async_copy(og_hbm, og_ref, lsem.at[1])
    load_w.start()
    load_og.start()

    def fill(c, carry):
        part = dot_nn(scatter_chunk(home_ref, c * QB, QB), ev_ref[...]).astype(BF16)
        outbox[pl.ds(c * group, group)] = part.reshape(group, cap, width)
        return carry

    lax.fori_loop(0, nq, fill, 0)
    pl.semaphore_wait(barrier, n - 1)
    start_exchange(n, me, outbox, inbox, ssem, rsem)
    inbox[me] = outbox[me]
    gather_matrix(dest_ref, pick)
    load_w.wait()
    load_og.wait()

    def prepare(c, carry):
        r = pl.ds(pl.multiple_of(c * QB, QB), QB)
        low = lax.broadcasted_iota(jnp.int32, (QB, rows), 0) + c * QB
        high = lax.broadcasted_iota(jnp.int32, (QB, rows), 1)
        low_col = lax.broadcasted_iota(jnp.int32, (QB, 1), 0) + c * QB
        high_row = lax.broadcasted_iota(jnp.int32, (1, rows), 1)
        q_own = owner_of(low_col, lens_ref, -1)
        k_own = owner_of(high_row, lens_ref, -2)
        mask[r, :] = jnp.where((q_own == k_own) & (high <= low), 1.0, 0.0).astype(BF16)
        mask_t[r, :] = jnp.where((q_own == k_own) & (low <= high), 1.0, 0.0).astype(BF16)
        dmix[r, :] = dot_nt(og_ref[r, :], w_ref[:, 4 * width :]).astype(BF16)
        return carry

    lax.fori_loop(0, nq, prepare, 0)
    finish_exchange(n, me, outbox, inbox, ssem, rsem)

    def project(c, carry):
        r = pl.ds(pl.multiple_of(c * QB, QB), QB)
        x = dot_nn(pick[r, :], inbox[...].reshape(rows, width)).astype(BF16)
        tok_ref[r, :] = x
        for g in range(4):
            cols = slice(g * width, (g + 1) * width)
            u = dot_nn(x, w_ref[:, cols]) * 0.5
            t = jnp.tanh(u)
            a = u * t + u
            slope[r, cols] = (0.5 * ((1.0 + a) + t * (1.0 - a))).astype(BF16)
            if g == 0:
                gate[r, :] = a
            elif g == 1:
                vs[r, :] = a.astype(BF16)
            elif g == 2:
                qs[r, :] = (a.astype(BF16).astype(F32) * (0.5 * (width // HEADS) ** -0.5)).astype(BF16)
            else:
                ks[r, :] = a.astype(BF16)
        return carry

    lax.fori_loop(0, nq, project, 0)

    pair_width = 128
    head = width // HEADS
    lane = lax.broadcasted_iota(jnp.int32, (1, pair_width), 1) // head
    picks = [jnp.where(lane == h, 1.0, 0.0).astype(BF16) for h in range(pair_width // head)]

    def forward(p, carry):
        cols = pl.ds(pl.multiple_of(p * pair_width, pair_width), pair_width)
        for c in range(nq):
            top = (c + 1) * QB
            r = slice(c * QB, top)
            out = None
            for sel in picks:
                u = dot_nt(qs[r, cols] * sel, ks[:top, cols])
                t = jnp.tanh(u)
                a = (u * t + u).astype(BF16) * mask[r, :top]
                o = dot_nn(a, vs[:top, cols] * sel)
                out = o if out is None else out + o
            att[r, cols] = out
        return carry

    lax.fori_loop(0, width // pair_width, forward, 0)

    def norm(c, carry):
        r = pl.ds(pl.multiple_of(c * QB, QB), QB)
        x = att[r, :]
        centred = x - jnp.mean(x, axis=1, keepdims=True)
        spread = jnp.mean(centred * centred, axis=1, keepdims=True)
        inv = lax.rsqrt(spread + NORM_EPS)
        unit = centred * inv
        g = gate[r, :]
        mixed[r, :] = (unit * g).astype(BF16)
        dm = dmix[r, :].astype(F32)
        hgrad[r, :width] = (dm * unit * slope[r, :width]).astype(BF16)
        dn = dm * g
        mean_a = jnp.mean(dn, axis=1, keepdims=True)
        mean_b = jnp.mean(dn * unit, axis=1, keepdims=True)
        dout[r, :] = (inv * (dn - mean_a - unit * mean_b)).astype(BF16)
        return carry

    lax.fori_loop(0, nq, norm, 0)

    pairs = width // pair_width
    sources = bufs[:4]
    hops = bufs[4:]
    sums = (f0_ref, f1_ref, f2_ref, f3_ref)

    def hop(chain, stage):
        bit = chain_bits(bits, chain % 2 == 1)[stage]
        mine = (me // (1 << bit)) % 2
        peer = me + (1 - 2 * mine) * (1 << bit)
        cur = sources[chain] if stage == 0 else hops[chain * bits + stage - 1]
        got = hops[chain * bits + stage]
        half = cur.shape[0] // 2
        copy = pltpu.make_async_remote_copy(
            src_ref=cur.at[pl.ds((1 - mine) * half, half)],
            dst_ref=got,
            send_sem=hs.at[chain * bits + stage],
            recv_sem=hr.at[chain * bits + stage],
            device_id=(peer,),
            device_id_type=MESH,
        )
        return copy, cur.at[pl.ds(mine * half, half)], got

    def advance(chain, stage):
        copy, kept, got = hop(chain, stage)
        copy.wait()
        total = kept[...].astype(F32) + got[...].astype(F32)
        if stage == bits - 1:
            sums[chain][...] = total
        else:
            got[...] = total.astype(BF16)
            hop(chain, stage + 1)[0].start()

    def weight_grad(chain, left, right, base, wide):
        thin = wide // fold
        height = n * per * fold
        order = chain_bits(bits, chain % 2 == 1)
        for turn in range(fold):
            tp[...] = dot_nt(
                order_matrix(height, width, n, per, order, fold, turn), left[...]
            ).astype(BF16)
            step = 256 if thin % 256 == 0 else thin
            for j in range(thin // step):
                start = base + turn * thin + j * step
                part = dot_nn(tp[...], right[:, start : start + step])
                cols = slice(j * step, (j + 1) * step)
                if turn == 0:
                    sources[chain][:, cols] = part.astype(BF16)
                else:
                    sources[chain][:, cols] += part.astype(BF16)
        hop(chain, 0)[0].start()

    weight_grad(0, tok_ref, hgrad, 0, width)
    weight_grad(1, mixed, og_ref, 0, width)

    def backward(p, carry):
        off = pl.multiple_of(p * pair_width, pair_width)
        cols = pl.ds(off, pair_width)
        for c in range(nq):
            top = (c + 1) * QB
            r = slice(c * QB, top)
            dq = None
            for sel in picks:
                qm = qs[r, cols] * sel
                dm = dout[r, cols] * sel
                u = dot_nt(ks[:top, cols], qm)
                t = jnp.tanh(u)
                a = u * t + u
                m = mask_t[:top, r]
                d = dot_nt(vs[:top, cols], dm)
                ds = (d * ((1.0 + a) + t * (1.0 - a))).astype(BF16) * m
                pb = a.astype(BF16) * m
                dv = dot_nn(pb, dm)
                dk = dot_nn(ds, qm)
                part = dot_tn(ds, ks[:top, cols] * sel)
                dq = part if dq is None else dq + part
                if c > 0:
                    acc_v[: c * QB, :] += dv[: c * QB]
                    acc_k[: c * QB, :] += dk[: c * QB]
                if sel is picks[0]:
                    acc_v[c * QB : top, :] = dv[c * QB :]
                    acc_k[c * QB : top, :] = dk[c * QB :]
                else:
                    acc_v[c * QB : top, :] += dv[c * QB :]
                    acc_k[c * QB : top, :] += dk[c * QB :]
            qcols = pl.ds(2 * width + off, pair_width)
            dq = (dq * (0.5 * head**-0.5)).astype(BF16).astype(F32)
            hgrad[r, qcols] = (dq * slope[r, qcols]).astype(BF16)
        vcols = pl.ds(width + off, pair_width)
        kcols = pl.ds(3 * width + off, pair_width)
        hgrad[:, vcols] = (acc_v[...].astype(BF16).astype(F32) * slope[:, vcols]).astype(BF16)
        hgrad[:, kcols] = (acc_k[...].astype(BF16).astype(F32) * slope[:, kcols]).astype(BF16)
        for s in range(min(pairs, bits - 1)):

            @pl.when(p == s)
            def _():
                for chain in (0, 1):
                    advance(chain, s)

        return carry

    lax.fori_loop(0, pairs, backward, 0)

    def tokens_back(c, carry):
        r = pl.ds(pl.multiple_of(c * QB, QB), QB)
        dout[r, :] = (
            og_ref[r, :].astype(F32) + dot_nt(hgrad[r, :], w_ref[:, : 4 * width])
        ).astype(BF16)
        return carry

    lax.fori_loop(0, nq, tokens_back, 0)

    def send_rows(c, carry):
        part = dot_nn(scatter_chunk(dest_ref, c * QB, QB), dout[...]).astype(BF16)
        outbox[pl.ds(c * group, group)] = part.reshape(group, cap, width)
        return carry

    lax.fori_loop(0, nq, send_rows, 0)
    start_exchange(n, me, outbox, inbox2, ssem2, rsem2)
    wide = 3 * width // 2
    weight_grad(2, tok_ref, hgrad, width, wide)
    weight_grad(3, tok_ref, hgrad, width + wide, wide)
    inbox2[me] = outbox[me]
    for stage in range(min(pairs, bits - 1), bits):
        advance(0, stage)
        advance(1, stage)
    for stage in range(bits):
        advance(2, stage)
        advance(3, stage)
    finish_exchange(n, me, outbox, inbox2, ssem2, rsem2)
    store = pltpu.make_async_copy(inbox2, ret_ref, lsem.at[0])
    store.start()
    store.wait()


def finish_kernel(scale, home_ref, ret_ref, fi_ref, fo_ref, mi_ref, mo_ref, ev_ref, ni_ref, no_ref, pick):
    rows, width = ev_ref.shape
    gather_matrix(home_ref, pick)
    step = 256
    back = ret_ref[...].reshape(rows, width)
    for c in range(rows // step):
        ev_ref[c * step : (c + 1) * step] = dot_nn(pick[c * step : (c + 1) * step], back).astype(BF16)
    cols = 0
    for ref in fi_ref:
        wide = ref.shape[1]
        ni_ref[:, cols : cols + wide] = DECAY * mi_ref[:, cols : cols + wide] + scale * ref[...]
        cols += wide
    no_ref[...] = DECAY * mo_ref[...] + scale * fo_ref[...]


def finish_entry(scale, home, ret, fa, fb, fc, fo, mi, mo, ev, ni, no, pick):
    finish_kernel(scale, home, ret, (fa, fb, fc), fo, mi, mo, ev, ni, no, pick)


def shards(n, events, home_slot, dest_slot, seq_lens, weights, out_grad, momentum_in, momentum_out):
    rows, width = events.shape
    cap = rows // n
    bits = n.bit_length() - 1
    per = width // n
    fold = max(1, 16 // per)
    tall = per * fold
    home = home_slot.reshape(1, rows)
    dest = dest_slot.reshape(1, rows)
    vm = pl.BlockSpec(memory_space=pltpu.VMEM)
    sm = pl.BlockSpec(memory_space=pltpu.SMEM)
    hbm = pl.BlockSpec(memory_space=pl.ANY)
    dma = pltpu.SemaphoreType.DMA
    wides = (width, width, 3 * width // 2, 3 * width // 2)
    thins = [w // fold for w in wides]
    bufs = [pltpu.VMEM((n * tall, t), BF16) for t in thins]
    for t in thins:
        for stage in range(bits):
            size = (n * tall >> (stage + 1), t)
            bufs.append(pltpu.VMEM(size, BF16))

    def area(r, c, kind=BF16):
        return pltpu.VMEM((r, c), kind)

    boxed = pltpu.VMEM((n, cap, width), BF16)
    ret, *parts = pl.pallas_call(
        functools.partial(step_kernel, n),
        out_shape=[jax.ShapeDtypeStruct((n, cap, width), BF16)]
        + [jax.ShapeDtypeStruct((tall, t), F32) for t in thins],
        in_specs=[sm, vm, vm, vm, hbm, hbm],
        out_specs=[hbm] + [vm] * 4,
        scratch_shapes=[
            area(width, 5 * width),
            area(rows, width),
            boxed,
            boxed,
            boxed,
            area(rows, rows),
            area(rows, width),
            area(rows, width),
            area(rows, 4 * width),
            area(rows, width, F32),
            area(rows, width),
            area(rows, width),
            area(rows, width),
            area(rows, width, F32),
            area(rows, 4 * width),
            area(rows, rows),
            area(rows, rows),
            area(rows, width),
            area(rows, width),
            area(rows, 128, F32),
            area(rows, 128, F32),
            area(n * tall, rows),
            dma((2,)),
            dma((n,)),
            dma((n,)),
            dma((n,)),
            dma((n,)),
            dma((4 * bits,)),
            dma((4 * bits,)),
        ]
        + bufs,
        compiler_params=pltpu.CompilerParams(
            collective_id=0, has_side_effects=True, vmem_limit_bytes=VMEM_LIMIT
        ),
        name="step",
    )(seq_lens, home, dest, events, weights, out_grad)
    f0, f1, f2, f3 = [
        f.reshape(fold, per, f.shape[1]).transpose(1, 0, 2).reshape(per, fold * f.shape[1])
        for f in parts
    ]
    return pl.pallas_call(
        functools.partial(finish_entry, (n * rows) ** (-0.5)),
        out_shape=[
            jax.ShapeDtypeStruct(events.shape, BF16),
            jax.ShapeDtypeStruct(momentum_in.shape, F32),
            jax.ShapeDtypeStruct(momentum_out.shape, F32),
        ],
        in_specs=[vm] * 8,
        out_specs=[vm] * 3,
        scratch_shapes=[pltpu.VMEM((rows, rows), BF16)],
        compiler_params=pltpu.CompilerParams(vmem_limit_bytes=VMEM_LIMIT),
        name="finish",
    )(home, ret, f0, f2, f3, f1, momentum_in, momentum_out)


def solution(mesh):
    n = mesh.shape["dp"]
    row = P("dp", None)
    return jax.shard_map(
        functools.partial(shards, n),
        mesh=mesh,
        in_specs=(row, P("dp"), P("dp"), P("dp"), P(), row, row, row),
        out_specs=(row, row, row),
        check_vma=False,
    )
```

profile of v0, /device:TPU:0, one launch (start us, length us, event | category | flops | bytes accessed | tf_op | source)
XLA Modules:
  0.0 111.3 jit_solution(10514380603753971814)
XLA Ops:
  0.6 107.0 %step.1 = (bf16[32,32,512]{2,1,0:T(8,128)(2,1)}, f32[16,512]{1,0:T(8,128)}, f32[16,512]{1,0:T(8,128)}, f32[16,768]{1,0:T(8,128)}, f32[16,768]{1,0:T(8,128)}) custom-call(s32[2]{0:T(128)} %lens_ref.1, s32[1,1024]{1,0:T(1,128)} %bitcast.2, s32[1,1024]{1,0:T(1,128)} %bitcast.4, bf16[1024,512]{1,0:T(8,128)(2,1)} %ev_ref.1, bf16[512,2560]{1,0:T(8,128)(2,1)} %w_hbm.1, ...), custom_call_target="tpu_custom_call" | custom-call | tf_op jit(solution)/shard_map/step/pallas_call | solution.py:414
  107.7 3.6 %finish.1 = (bf16[1024,512]{1,0:T(8,128)(2,1)}, f32[16,2048]{1,0:T(8,128)}, f32[16,512]{1,0:T(8,128)}) custom-call(s32[1,1024]{1,0:T(1,128)} %bitcast.3, bf16[32,32,512]{2,1,0:T(8,128)(2,1)} %get-tuple-element.8.ret, f32[16,512]{1,0:T(8,128)} %get-tuple-element.9.fa, f32[16,768]{1,0:T(8,128)} %get-tuple-element.10.fb, f32[16,768]{1,0:T(8,128)} %get-tuple-element.11.fc, ...), custom_call_target="tpu_custom_call" | custom-call | tf_op jit(solution)/shard_map/finish/pallas_call | solution.py:461
where the time goes:
time: 113 us; the launch traced here: 111 us
  Pallas kernels  111 us (98%)
    pallas_call x1, Pallas kernels, shards(): pl.pallas_call(functools.partial(step_kernel, n), out_shape=[jax.ShapeDty...  107 us
    pallas_call x1, Pallas kernels, shards(): pl.pallas_call(functools.partial(finish_entry, (n * rows) ** (-0.5)), out...  3.65 us

commit v1 on v0

v1 whole, which is shorter than its diff:
```python
import functools

import jax
import jax.numpy as jnp
from jax import lax
from jax.experimental import pallas as pl
from jax.experimental.pallas import tpu as pltpu
from jax.sharding import PartitionSpec as P

HEADS = 8
BLK = 512
QB = 256
PAIR = 128
NORM_EPS = 1e-05
DECAY = 0.9
MESH = pl.DeviceIdType.MESH
F32 = jnp.float32
BF16 = jnp.bfloat16
VMEM_LIMIT = 67 * 1000 * 1000
LAG = 2


def dot_nn(a, b):
    return lax.dot_general(a, b, (((1,), (0,)), ((), ())), preferred_element_type=F32)


def dot_nt(a, b):
    return lax.dot_general(a, b, (((1,), (1,)), ((), ())), preferred_element_type=F32)


def chain_bits(bit_count, second):
    order = list(range(bit_count))
    if second and bit_count > 2:
        order[1], order[2] = order[2], order[1]
    return order


def slot_device(slot, n, bits):
    return sum(((slot // (n >> (rank + 1))) % 2) << bit for rank, bit in enumerate(bits))


def enter_all(n, me):
    barrier = pltpu.get_barrier_semaphore()

    def greet(i, carry):
        pl.semaphore_signal(barrier, inc=1, device_id=((me + i) % n,), device_id_type=MESH)
        return carry

    lax.fori_loop(1, n, greet, 0)
    return barrier


def flip(value, other, size):
    total = 0
    weight = 1
    while weight < size:
        total = total + (value // weight + other // weight) % 2 * weight
        weight *= 2
    return total


class Exchange:
    def __init__(self, n, me, group, src, dst, ssem, rsem):
        self.n, self.me, self.group = n, me, group
        self.src, self.dst, self.ssem, self.rsem = src, dst, ssem, rsem

    def chunk(self, k):
        return flip(self.me // self.group, k, self.n // self.group)

    def each(self, k, act):
        base = self.chunk(k) * self.group
        low = self.me % self.group

        def go(j, carry):
            peer = base + flip(low, j, self.group)
            i = k * self.group + j
            act(
                pltpu.make_async_remote_copy(
                    src_ref=self.src.at[peer],
                    dst_ref=self.dst.at[self.me],
                    send_sem=self.ssem.at[i],
                    recv_sem=self.rsem.at[i],
                    device_id=(peer,),
                    device_id_type=MESH,
                )
            )
            return carry

        lax.fori_loop(1 if k == 0 else 0, self.group, go, 0)

    def start(self, k):
        self.each(k, lambda copy: copy.start())

    def finish(self, k):
        self.each(k, lambda copy: copy.wait())


def gather_matrix(slots_ref, out_ref):
    rows = out_ref.shape[0]
    wide = jnp.broadcast_to(slots_ref[...].astype(F32), (128, rows))
    column = jnp.transpose(wide)
    lane = lax.broadcasted_iota(jnp.int32, (rows, 128), 1).astype(F32)
    for j in range(rows // 128):
        out_ref[:, j * 128 : (j + 1) * 128] = jnp.where(
            column == lane + float(j * 128), 1.0, 0.0
        ).astype(BF16)


def scatter_chunk(slots_ref, start, size):
    rows = slots_ref.shape[1]
    place = lax.broadcasted_iota(jnp.int32, (size, rows), 0) + start
    return jnp.where(place == slots_ref[...], 1.0, 0.0).astype(BF16)


def same_owner(lens_ref, low, high):
    start = 0
    same = 0
    for j in range(lens_ref.shape[0]):
        blocks = (lens_ref[j] + BLK - 1) // BLK
        inside = jnp.where((start <= low) & (high < start + blocks), 1, 0)
        same = same + inside
        start = start + blocks
    return same


def order_block(height, base, width, n, per, bits, fold, turn):
    shape = (height, width)
    tall = per * fold
    place = lax.broadcasted_iota(jnp.int32, shape, 0) + base
    column = lax.broadcasted_iota(jnp.int32, shape, 1)
    slot = place // tall
    rest = place % tall
    device = jnp.zeros(shape, jnp.int32)
    for rank, bit in enumerate(bits):
        weight = n >> (rank + 1)
        device = device + ((slot // weight) % 2) * (1 << bit)
    hit = (column == device * per + rest % per) & (rest // per == turn)
    return jnp.where(hit, 1.0, 0.0).astype(BF16)


def step_kernel(n, scale, direct, lens_ref, home_ref, dest_ref, ev_ref, w_hbm, og_hbm, *refs):
    if direct:
        mi_ref, mo_ref, out_ev, ni_ref, no_ref, *refs = refs
        sums = None
    else:
        out_ev, *refs = refs
        sums, refs = refs[:4], refs[4:]
    (
        w_ref, og_ref, og_t, outbox, inbox, inbox2, pick, place, tok, tok_t, dmix_t,
        slope_t, gate_t, v_t, q_t, k_t, k_z, v_z, attn, slopes, att_t, hgrad_t, mixed_t,
        dout_t, acc, cross, lsem, ssem, rsem, ssem2, rsem2, hs, hr, *bufs,
    ) = refs
    me = lax.axis_index("dp")
    rows, width = ev_ref.shape
    cap = rows // n
    per = width // n
    fold = max(1, 16 // per)
    nq = rows // QB
    bits = n.bit_length() - 1
    group = QB // cap
    head = width // HEADS
    pairs = width // PAIR
    two = PAIR // head
    barrier = enter_all(n, me)
    load_w = pltpu.make_async_copy(w_hbm, w_ref, lsem.at[0])
    load_og = pltpu.make_async_copy(og_hbm, og_ref, lsem.at[1])
    load_w.start()
    load_og.start()
    there = Exchange(n, me, group, outbox, inbox, ssem, rsem)
    back = Exchange(n, me, group, outbox, inbox2, ssem2, rsem2)

    for k in range(nq):
        at = there.chunk(k)
        part = dot_nn(scatter_chunk(home_ref, at * QB, QB), ev_ref[...]).astype(BF16)
        outbox[pl.ds(at * group, group)] = part.reshape(group, cap, width)
        if k == 0:
            pl.semaphore_wait(barrier, n - 1)
        there.start(k)
    inbox[me] = outbox[me]
    gather_matrix(dest_ref, pick)
    load_w.wait()
    load_og.wait()

    def prepare(c, carry):
        r = pl.ds(pl.multiple_of(c * QB, QB), QB)
        place[r, :] = scatter_chunk(dest_ref, c * QB, QB)
        x = og_ref[r, :]
        og_t[:, r] = jnp.transpose(x)
        dmix_t[:, r] = (dot_nt(w_ref[:, 4 * width :], x) * 0.5).astype(BF16)
        return carry

    lax.fori_loop(0, nq, prepare, 0)

    def turn_w(c, carry):
        r = pl.ds(pl.multiple_of(c * QB, QB), QB)
        hgrad_t[r, :width] = jnp.transpose(w_ref[:, r]) * 0.5
        return carry

    lax.fori_loop(0, 4 * width // QB, turn_w, 0)

    blocks = rows // BLK
    links = [(i, j) for i in range(blocks) for j in range(i)]
    for x, (i, j) in enumerate(links):
        cross[x] = jnp.full((PAIR, QB), same_owner(lens_ref, j, i), jnp.int32).astype(F32).astype(BF16)

    def linked(value, qc, kc):
        i, j = qc * QB // BLK, kc * QB // BLK
        return value if i == j else value * cross[links.index((i, j))]

    for k in range(nq):
        there.finish(k)
        at = there.chunk(k)
        box = inbox[pl.ds(at * group, group)].reshape(QB, width)
        part = dot_nn(pick[:, pl.ds(pl.multiple_of(at * QB, QB), QB)], box).astype(BF16)
        if k == 0:
            tok[...] = part
        else:
            tok[...] += part

    lane = lax.broadcasted_iota(jnp.int32, (1, PAIR), 1) // head
    picks = [jnp.where(lane == h, 1.0, 0.0).astype(BF16) for h in range(two)]

    def project(c, carry):
        r = pl.ds(pl.multiple_of(c * QB, QB), QB)
        x = tok[r, :]
        for g in range(4):
            rs = slice(g * width, (g + 1) * width)
            u = dot_nt(hgrad_t[rs, :width], x)
            w = jnp.tanh(u) + 1.0
            a = u * w
            low = a.astype(BF16)
            wb = w.astype(BF16)
            slope_t[rs, r] = wb + low * (2.0 - wb)
            if g == 0:
                gate_t[:, r] = low
            elif g == 2:
                q_t[:, :, r] = (low * (0.5 * head**-0.5)).reshape(pairs, PAIR, QB)
            else:
                here, flat = (v_t, v_z) if g == 1 else (k_t, k_z)
                here[:, :, r] = low.reshape(HEADS, head, QB)
                for p in range(pairs):
                    tall = jnp.transpose(low[p * PAIR : (p + 1) * PAIR])
                    for h in range(two):
                        flat[p * two + h, r, :] = tall * picks[h]
        return carry

    lax.fori_loop(0, nq, project, 0)

    tiles = [(qc, kc) for qc in range(nq) for kc in range(qc + 1)]
    low_i = lax.broadcasted_iota(jnp.int32, (QB, QB), 0)
    high_i = lax.broadcasted_iota(jnp.int32, (QB, QB), 1)

    def span(c):
        return slice(c * QB, (c + 1) * QB)

    def forward(p, carry):
        tri = jnp.where(low_i <= high_i, 1.0, 0.0).astype(BF16)
        work = [(h, qc, kc) for h in range(two) for qc, kc in tiles]
        held = {}
        out = None
        for i in range(len(work) + LAG):
            if i < len(work):
                h, qc, kc = work[i]
                q = linked(q_t[p, :, span(qc)], qc, kc)
                held[i] = dot_nn(k_z[p * two + h, span(kc), :], q)
            if i < LAG:
                continue
            h, qc, kc = work[i - LAG]
            u = held.pop(i - LAG)
            g = p * two + h
            w = jnp.tanh(u) + 1.0
            a = (u * w).astype(BF16)
            wb = w.astype(BF16)
            s = wb + a * (2.0 - wb)
            if qc == kc:
                a = a * tri
                s = s * tri
            attn[g, tiles.index((qc, kc))] = a
            slopes[g, tiles.index((qc, kc))] = s
            o = dot_nn(v_t[g, :, span(kc)], a)
            out = o if kc == 0 else out + o
            if qc == kc:
                att_t[g, :, span(qc)] = out
        return carry

    lax.fori_loop(0, pairs, forward, 0)

    def norm(c, carry):
        r = pl.ds(pl.multiple_of(c * 128, 128), 128)
        x = att_t[:, :, r].reshape(width, 128)
        centred = x - jnp.mean(x, axis=0, keepdims=True)
        spread = jnp.mean(centred * centred, axis=0, keepdims=True)
        inv = lax.rsqrt(spread + NORM_EPS)
        unit = centred * inv
        g = gate_t[:, r].astype(F32)
        mixed_t[:, r] = (unit * g).astype(BF16)
        dm = dmix_t[:, r].astype(F32)
        hgrad_t[:width, r] = (dm * unit * slope_t[:width, r].astype(F32)).astype(BF16)
        dn = dm * g
        mean_a = jnp.mean(dn, axis=0, keepdims=True)
        mean_b = jnp.mean(dn * unit, axis=0, keepdims=True)
        dout_t[:, :, r] = (
            (inv * (dn - mean_a - unit * mean_b)).astype(BF16).reshape(pairs, PAIR, 128)
        )
        return carry

    lax.fori_loop(0, rows // 128, norm, 0)

    sources = bufs[:4]
    hops = bufs[4:]

    def hop(chain, stage):
        bit = chain_bits(bits, chain % 2 == 1)[stage]
        mine = (me // (1 << bit)) % 2
        peer = me + (1 - 2 * mine) * (1 << bit)
        cur = sources[chain] if stage == 0 else hops[chain * bits + stage - 1]
        got = hops[chain * bits + stage]
        half = cur.shape[0] // 2
        copy = pltpu.make_async_remote_copy(
            src_ref=cur.at[pl.ds((1 - mine) * half, half)],
            dst_ref=got,
            send_sem=hs.at[chain * bits + stage],
            recv_sem=hr.at[chain * bits + stage],
            device_id=(peer,),
            device_id_type=MESH,
        )
        return copy, cur.at[pl.ds(mine * half, half)], got

    half_w = width // 2
    wide = 3 * half_w
    if direct:
        columns = [
            [(0, width)],
            None,
            [(width * g, half_w) for g in (1, 2, 3)],
            [(width * g + half_w, half_w) for g in (1, 2, 3)],
        ]
    else:
        columns = [[(0, width)], None, [(width, wide)], [(width + wide, wide)]]

    def advance(chain, stage):
        copy, kept, got = hop(chain, stage)
        copy.wait()
        total = kept[...].astype(F32) + got[...].astype(F32)
        if stage < bits - 1:
            got[...] = total.astype(BF16)
            hop(chain, stage + 1)[0].start()
        elif not direct:
            sums[chain][...] = total
        elif chain == 1:
            no_ref[...] = DECAY * mo_ref[...] + scale * total
        else:
            at = 0
            for start, size in columns[chain]:
                cols = slice(start, start + size)
                ni_ref[:, cols] = DECAY * mi_ref[:, cols] + scale * total[:, at : at + size]
                at += size

    def weight_grad(chain):
        order = chain_bits(bits, chain % 2 == 1)
        if direct:
            at = 0
            for start, size in columns[chain] or [(0, width)]:
                for j in range(0, size, QB):
                    lo = start + j
                    if chain == 1:
                        part = dot_nn(mixed_t[...], og_ref[:, lo : lo + QB])
                    else:
                        part = dot_nt(tok_t[...], hgrad_t[lo : lo + QB, :])
                    part = part.astype(BF16)
                    for slot in range(n):
                        d = slot_device(slot, n, order)
                        sources[chain][slot * per : (slot + 1) * per, at : at + QB] = part[
                            d * per : (d + 1) * per
                        ]
                    at += QB
        else:
            base, size = (columns[chain] or [(0, width)])[0]
            thin = size // fold
            step = QB if thin % QB == 0 else thin
            strip = 128

            def fold_rows(x, carry):
                lo = pl.multiple_of(x * strip, strip)
                spot = pl.ds(lo, strip)
                for turn in range(fold):
                    mat = order_block(strip, lo, width, n, per, order, fold, turn)
                    if chain == 1:
                        left = dot_nn(mat, mixed_t[...]).astype(BF16)
                    else:
                        left = dot_nt(mat, tok[...]).astype(BF16)
                    for j in range(thin // step):
                        start = base + turn * thin + j * step
                        if chain == 1:
                            part = dot_nn(left, og_ref[:, start : start + step])
                        else:
                            part = dot_nt(left, hgrad_t[start : start + step, :])
                        cols = slice(j * step, (j + 1) * step)
                        if turn == 0:
                            sources[chain][spot, cols] = part.astype(BF16)
                        else:
                            sources[chain][spot, cols] += part.astype(BF16)
                return carry

            lax.fori_loop(0, n * per * fold // strip, fold_rows, 0)
        hop(chain, 0)[0].start()

    if direct:
        for c in range(nq):
            tok_t[:, span(c)] = jnp.transpose(tok[span(c), :])
    weight_grad(0)
    weight_grad(1)

    def backward(p, carry):
        work = [(h, qc, kc) for h in range(two) for kc in range(nq) for qc in range(kc, nq)]
        held = {}
        dk = dv = None
        for i in range(len(work) + LAG):
            if i < len(work):
                h, qc, kc = work[i]
                d = linked(dout_t[p, :, span(qc)], qc, kc)
                held[i] = dot_nn(v_z[p * two + h, span(kc), :], d)
            if i < LAG:
                continue
            h, qc, kc = work[i - LAG]
            u = held.pop(i - LAG)
            g = p * two + h
            t = tiles.index((qc, kc))
            hr_ = slice(h * head, (h + 1) * head)
            ds = u.astype(BF16) * slopes[g, t]
            dq = dot_nn(k_t[g, :, span(kc)], ds)
            if kc == 0:
                acc[h, :, span(qc)] = dq
            else:
                acc[h, :, span(qc)] += dq
            one = dot_nt(q_t[p, hr_, span(qc)], ds)
            two_ = dot_nt(dout_t[p, hr_, span(qc)], attn[g, t])
            dk = one if qc == kc else dk + one
            dv = two_ if qc == kc else dv + two_
            if qc == nq - 1:
                for grp, val in ((1, dv), (3, dk)):
                    rs = pl.ds(pl.multiple_of(grp * width + p * PAIR + h * head, head), head)
                    hgrad_t[rs, span(kc)] = (
                        val.astype(BF16).astype(F32) * slope_t[rs, span(kc)].astype(F32)
                    ).astype(BF16)
            if kc == qc:
                rs = pl.ds(pl.multiple_of(2 * width + p * PAIR + h * head, head), head)
                full = (acc[h, :, span(qc)] * (0.5 * head**-0.5)).astype(BF16).astype(F32)
                hgrad_t[rs, span(qc)] = (full * slope_t[rs, span(qc)].astype(F32)).astype(BF16)

        @pl.when(p == 0)
        def _():
            advance(0, 0)
            advance(1, 0)

        if direct:

            @pl.when(p == pairs // 2 - 1)
            def _():
                weight_grad(2)

        @pl.when(p == pairs - 2)
        def _():
            advance(0, 1)
            advance(1, 1)

        @pl.when(p == pairs - 1)
        def _():
            if direct:
                advance(2, 0)
            advance(0, 2)
            advance(1, 2)

        return carry

    lax.fori_loop(0, pairs, backward, 0)

    def tokens_back(c, carry):
        r = pl.ds(pl.multiple_of(c * QB, QB), QB)
        dmix_t[:, r] = (
            og_t[:, r].astype(F32) + dot_nn(w_ref[:, : 4 * width], hgrad_t[:, r])
        ).astype(BF16)
        return carry

    lax.fori_loop(0, nq, tokens_back, 0)

    for k in range(nq):
        at = back.chunk(k)
        r = pl.ds(pl.multiple_of(at * QB, QB), QB)
        part = dot_nt(place[r, :], dmix_t[...]).astype(BF16)
        outbox[pl.ds(at * group, group)] = part.reshape(group, cap, width)
        back.start(k)
    if not direct:
        weight_grad(2)
    weight_grad(3)
    inbox2[me] = outbox[me]
    gather_matrix(home_ref, pick)
    if not direct:
        advance(2, 0)
    for stage in range(bits):
        if stage >= 3:
            advance(0, stage)
            advance(1, stage)
        if stage >= 1:
            advance(2, stage)
        advance(3, stage)
    for k in range(nq):
        back.finish(k)
        at = back.chunk(k)
        box = inbox2[pl.ds(at * group, group)].reshape(QB, width)
        part = dot_nn(pick[:, pl.ds(pl.multiple_of(at * QB, QB), QB)], box).astype(BF16)
        if k == 0:
            tok[...] = part
        elif k < nq - 1:
            tok[...] += part
        else:
            out_ev[...] = tok[...] + part


def shards(n, events, home_slot, dest_slot, seq_lens, weights, out_grad, momentum_in, momentum_out):
    rows, width = events.shape
    cap = rows // n
    bits = n.bit_length() - 1
    per = width // n
    fold = max(1, 16 // per)
    tall = per * fold
    direct = fold == 1
    nq = rows // QB
    pairs = width // PAIR
    head = width // HEADS
    scale = (n * rows) ** (-0.5)
    home = home_slot.reshape(1, rows)
    dest = dest_slot.reshape(1, rows)
    vm = pl.BlockSpec(memory_space=pltpu.VMEM)
    sm = pl.BlockSpec(memory_space=pltpu.SMEM)
    hbm = pl.BlockSpec(memory_space=pl.ANY)
    dma = pltpu.SemaphoreType.DMA
    wides = (width, width, 3 * width // 2, 3 * width // 2)
    thins = [w // fold for w in wides]
    bufs = [pltpu.VMEM((n * tall, t), BF16) for t in thins]
    for t in thins:
        for stage in range(bits):
            bufs.append(pltpu.VMEM((n * tall >> (stage + 1), t), BF16))

    def area(*shape, kind=BF16):
        return pltpu.VMEM(shape, kind)

    boxed = area(n, cap, width)
    ntile = nq * (nq + 1) // 2
    blocks = rows // BLK
    ev_shape = jax.ShapeDtypeStruct(events.shape, BF16)
    if direct:
        outs = [
            ev_shape,
            jax.ShapeDtypeStruct(momentum_in.shape, F32),
            jax.ShapeDtypeStruct(momentum_out.shape, F32),
        ]
        more = (momentum_in, momentum_out)
    else:
        outs = [ev_shape] + [jax.ShapeDtypeStruct((tall, t), F32) for t in thins]
        more = ()
    got = pl.pallas_call(
        functools.partial(step_kernel, n, scale, direct),
        out_shape=outs,
        in_specs=[sm, vm, vm, vm, hbm, hbm] + [vm] * len(more),
        out_specs=[vm] * len(outs),
        scratch_shapes=[
            area(width, 5 * width),
            area(rows, width),
            area(width, rows),
            boxed,
            boxed,
            boxed,
            area(rows, rows),
            area(rows, rows),
            area(rows, width),
            area(width, rows),
            area(width, rows),
            area(4 * width, rows),
            area(width, rows),
            area(HEADS, head, rows),
            area(pairs, PAIR, rows),
            area(HEADS, head, rows),
            area(HEADS, rows, PAIR),
            area(HEADS, rows, PAIR),
            area(HEADS, ntile, QB, QB),
            area(HEADS, ntile, QB, QB),
            area(HEADS, head, rows, kind=F32),
            area(4 * width, rows),
            area(width, rows),
            area(pairs, PAIR, rows),
            area(PAIR // head, head, rows, kind=F32),
            area(max(1, blocks * (blocks - 1) // 2), PAIR, QB),
            dma((2,)),
            dma((n,)),
            dma((n,)),
            dma((n,)),
            dma((n,)),
            dma((4 * bits,)),
            dma((4 * bits,)),
        ]
        + bufs,
        compiler_params=pltpu.CompilerParams(
            collective_id=0, has_side_effects=True, vmem_limit_bytes=VMEM_LIMIT
        ),
        name="step",
    )(seq_lens, home, dest, events, weights, out_grad, *more)
    if direct:
        return tuple(got)
    ev, *parts = got
    f0, f1, f2, f3 = [
        f.reshape(fold, per, f.shape[1]).transpose(1, 0, 2).reshape(per, fold * f.shape[1])
        for f in parts
    ]
    return (
        ev,
        DECAY * momentum_in + scale * jnp.concatenate([f0, f2, f3], axis=1),
        DECAY * momentum_out + scale * f1,
    )


def solution(mesh):
    n = mesh.shape["dp"]
    row = P("dp", None)
    return jax.shard_map(
        functools.partial(shards, n),
        mesh=mesh,
        in_specs=(row, P("dp"), P("dp"), P("dp"), P(), row, row, row),
        out_specs=(row, row, row),
        check_vma=False,
    )
```

time: 113 us -> 105 us (0.929); the launches traced: 111 us -> 105 us
  Pallas kernels: 111 us -> 99.2 us
  local copies, waits for them, and re-layouts: 0 us -> 5.2 us
    pallas_call x2 -> x1, Pallas kernels: 111 us -> 99.2 us  [shards(): pl.pallas_call(functools.partial(step_kernel, n, scale, direct), out_shap...]
    unnamed x0 -> x3, local copies, waits for them, and re-layouts: none -> 5.2 us
where the time goes in v1:
time: 105 us
  Pallas kernels  99.2 us (94%)
  local copies, waits for them, and re-layouts  5.2 us (5%)
    pallas_call x1, Pallas kernels, shards(): pl.pallas_call(functools.partial(step_kernel, n, scale, direct), out_shap...  99.2 us
    unnamed x3, local copies, waits for them, and re-layouts  5.2 us

profile of v1, /device:TPU:0, one launch (start us, length us, event | category | flops | bytes accessed | tf_op | source)
XLA Modules:
  0.0 105.1 jit_solution(3332294976923313172)
XLA Ops:
  0.6 99.2 %step.1 = (bf16[1024,512]{1,0:T(8,128)(2,1)}, f32[16,2048]{1,0:T(8,128)}, f32[16,512]{1,0:T(8,128)}) custom-call(s32[2]{0:T(128)} %lens_ref.1, s32[1,1024]{1,0:T(1,128)} %bitcast.2, s32[1,1024]{1,0:T(1,128)} %bitcast.3, bf16[1024,512]{1,0:T(8,128)(2,1)} %ev_ref.1, bf16[512,2560]{1,0:T(8,128)(2,1)} %w_hbm.1, bf16[1024,512]{1,0:T(8,128)(2,1)} %og_hbm.1, ...), custom_call_target="tpu_custom_call" | custom-call | tf_op jit(solution)/shard_map/step/pallas_call | solution.py:562
  99.9 2.3 %copy.14 = bf16[1024,512]{1,0:T(8,128)(2,1)} copy(bf16[1024,512]{1,0:T(8,128)(2,1)} %get-tuple-element.6) | data formatting | bytes 2097152
  102.1 1.6 %copy.15 = f32[16,2048]{1,0:T(8,128)} copy(f32[16,2048]{1,0:T(8,128)} %get-tuple-element.7) | data formatting | bytes 262144
  103.7 1.4 %copy.16 = f32[16,512]{1,0:T(8,128)} copy(f32[16,512]{1,0:T(8,128)} %get-tuple-element.8) | data formatting | bytes 65536

commit v2 on v1

--- a/solution.py
+++ b/solution.py
@@ -18,6 +18,19 @@
 BF16 = jnp.bfloat16
 VMEM_LIMIT = 67 * 1000 * 1000
 LAG = 2
+LATE = ((4, 0), (3, 1), (2, 2), (4, 1), (0, 4), (1, 4), (3, 2), (2, 3), (4, 2), (3, 3), (2, 4), (4, 3), (3, 4), (4, 4))
+PLAN = (('fill', 3), ('fill', 1), ('msg', 3, 0), ('msg', 1, 0), ('msg', 3, 1), ('msg', 1, 1), ('msg', 3, 2), ('msg', 1, 2), ('msg', 3, 3), ('msg', 1, 3), ('fill', 2), ('fill', 0), ('own',), ('msg', 3, 4), ('msg', 1, 4), ('msg', 3, 5), ('msg', 1, 5), ('grad', 4), ('gone', 3, 0), ('gone', 1, 0), ('msg', 3, 6), ('msg', 1, 6), ('add', 3, 1), ('add', 2, 2), ('gone', 3, 1), ('gone', 1, 1), ('msg', 3, 7), ('msg', 1, 7), ('add', 4, 0), ('gone', 3, 2), ('gone', 1, 2), ('msg', 2, 0), ('msg', 0, 1), ('add', 0, 4), ('add', 1, 4), ('gone', 3, 3), ('gone', 1, 3), ('msg', 2, 1), ('msg', 0, 2), ('add', 4, 1), ('add', 3, 2), ('gone', 3, 4), ('gone', 1, 4), ('msg', 2, 2), ('msg', 0, 3), ('add', 2, 3), ('gone', 3, 5), ('gone', 1, 5), ('msg', 2, 3), ('msg', 0, 4), ('add', 4, 2), ('add', 3, 3), ('gone', 3, 6), ('gone', 1, 6), ('msg', 2, 4), ('msg', 0, 5), ('gone', 3, 7), ('gone', 1, 7), ('msg', 2, 5), ('msg', 0, 6), ('add', 2, 4), ('add', 4, 3), ('add', 3, 4), ('gone', 2, 0), ('gone', 0, 1), ('msg', 2, 6), ('msg', 0, 7), ('gone', 2, 1), ('gone', 0, 2), ('msg', 2, 7), ('add', 4, 4), ('pick',), ('get', 0), ('get', 1), ('get', 2), ('get', 3), ('gone', 2, 2), ('gone', 0, 3), ('gone', 2, 3), ('gone', 0, 4), ('gone', 2, 4), ('gone', 0, 5), ('gone', 2, 5), ('gone', 0, 6), ('gone', 2, 6), ('gone', 0, 7), ('gone', 2, 7))
+WHOLE_PLAN = (
+    *((what, k) for k in range(4) for what in ("fill", "start")),
+    ("grad", 2),
+    ("grad", 3),
+    ("pick",),
+    *(("add", chain, stage) for stage in (3, 4, 5, 6) for chain in (0, 1)),
+    *(("add", chain, stage) for stage in range(7) for chain in (2, 3)),
+    ("own",),
+    *(("get", k) for k in range(4)),
+    *(("sent", k) for k in range(4)),
+)
 
 
 def dot_nn(a, b):
@@ -67,29 +80,33 @@
     def chunk(self, k):
         return flip(self.me // self.group, k, self.n // self.group)
 
+    def copy(self, k, j):
+        peer = self.chunk(k) * self.group + flip(self.me % self.group, j, self.group)
+        i = k * self.group + j
+        return pltpu.make_async_remote_copy(
+            src_ref=self.src.at[peer],
+            dst_ref=self.dst.at[self.me],
+            send_sem=self.ssem.at[i],
+            recv_sem=self.rsem.at[i],
+            device_id=(peer,),
+            device_id_type=MESH,
+        )
+
     def each(self, k, act):
-        base = self.chunk(k) * self.group
-        low = self.me % self.group
-
         def go(j, carry):
-            peer = base + flip(low, j, self.group)
-            i = k * self.group + j
-            act(
-                pltpu.make_async_remote_copy(
-                    src_ref=self.src.at[peer],
-                    dst_ref=self.dst.at[self.me],
-                    send_sem=self.ssem.at[i],
-                    recv_sem=self.rsem.at[i],
-                    device_id=(peer,),
-                    device_id_type=MESH,
-                )
-            )
+            act(self.copy(k, j))
             return carry
 
         lax.fori_loop(1 if k == 0 else 0, self.group, go, 0)
 
     def start(self, k):
         self.each(k, lambda copy: copy.start())
+
+    def sent(self, k):
+        self.each(k, lambda copy: copy.wait_send())
+
+    def arrived(self, k):
+        self.each(k, lambda copy: copy.wait_recv())
 
     def finish(self, k):
         self.each(k, lambda copy: copy.wait())
@@ -138,14 +155,11 @@
     return jnp.where(hit, 1.0, 0.0).astype(BF16)
 
 
-def step_kernel(n, scale, direct, lens_ref, home_ref, dest_ref, ev_ref, w_hbm, og_hbm, *refs):
-    if direct:
-        mi_ref, mo_ref, out_ev, ni_ref, no_ref, *refs = refs
-        sums = None
-    else:
-        out_ev, *refs = refs
-        sums, refs = refs[:4], refs[4:]
+def step_kernel(n, direct, lens_hbm, home_hbm, dest_hbm, ev_hbm, w_hbm, og_hbm, *refs):
+    chains = 5 if direct else 4
+    out_ev, sums, refs = refs[0], refs[1 : 1 + chains], refs[1 + chains :]
     (
+        lens_ref, home_ref, dest_ref, ev_ref,
         w_ref, og_ref, og_t, outbox, inbox, inbox2, pick, place, tok, tok_t, dmix_t,
         slope_t, gate_t, v_t, q_t, k_t, k_z, v_z, attn, slopes, att_t, hgrad_t, mixed_t,
         dout_t, acc, cross, lsem, ssem, rsem, ssem2, rsem2, hs, hr, *bufs,
@@ -162,10 +176,23 @@
     pairs = width // PAIR
     two = PAIR // head
     barrier = enter_all(n, me)
-    load_w = pltpu.make_async_copy(w_hbm, w_ref, lsem.at[0])
-    load_og = pltpu.make_async_copy(og_hbm, og_ref, lsem.at[1])
-    load_w.start()
-    load_og.start()
+    loads = [
+        pltpu.make_async_copy(src, dst, lsem.at[i])
+        for i, (src, dst) in enumerate(
+            (
+                (home_hbm, home_ref),
+                (ev_hbm, ev_ref),
+                (dest_hbm, dest_ref),
+                (og_hbm, og_ref),
+                (w_hbm, w_ref),
+                (lens_hbm, lens_ref),
+            )
+        )
+    ]
+    for load in loads:
+        load.start()
+    loads[0].wait()
+    loads[1].wait()
     there = Exchange(n, me, group, outbox, inbox, ssem, rsem)
     back = Exchange(n, me, group, outbox, inbox2, ssem2, rsem2)
 
@@ -177,9 +204,9 @@
             pl.semaphore_wait(barrier, n - 1)
         there.start(k)
     inbox[me] = outbox[me]
+    for load in loads[2:]:
+        load.wait()
     gather_matrix(dest_ref, pick)
-    load_w.wait()
-    load_og.wait()
 
     def prepare(c, carry):
         r = pl.ds(pl.multiple_of(c * QB, QB), QB)
@@ -271,12 +298,11 @@
             w = jnp.tanh(u) + 1.0
             a = (u * w).astype(BF16)
             wb = w.astype(BF16)
-            s = wb + a * (2.0 - wb)
             if qc == kc:
                 a = a * tri
-                s = s * tri
+                wb = wb * tri
             attn[g, tiles.index((qc, kc))] = a
-            slopes[g, tiles.index((qc, kc))] = s
+            slopes[g, tiles.index((qc, kc))] = wb
             o = dot_nn(v_t[g, :, span(kc)], a)
             out = o if kc == 0 else out + o
             if qc == kc:
@@ -306,11 +332,12 @@
 
     lax.fori_loop(0, rows // 128, norm, 0)
 
-    sources = bufs[:4]
-    hops = bufs[4:]
+    sources = bufs[:chains]
+    hops = bufs[chains:]
+    orders = [chain_bits(bits, chain in (1, 2)) for chain in range(chains)]
 
     def hop(chain, stage):
-        bit = chain_bits(bits, chain % 2 == 1)[stage]
+        bit = orders[chain][stage]
         mine = (me // (1 << bit)) % 2
         peer = me + (1 - 2 * mine) * (1 << bit)
         cur = sources[chain] if stage == 0 else hops[chain * bits + stage - 1]
@@ -326,56 +353,39 @@
         )
         return copy, cur.at[pl.ds(mine * half, half)], got
 
-    half_w = width // 2
-    wide = 3 * half_w
-    if direct:
-        columns = [
-            [(0, width)],
-            None,
-            [(width * g, half_w) for g in (1, 2, 3)],
-            [(width * g + half_w, half_w) for g in (1, 2, 3)],
-        ]
-    else:
-        columns = [[(0, width)], None, [(width, wide)], [(width + wide, wide)]]
+    columns = chain_columns(width, direct)
 
     def advance(chain, stage):
         copy, kept, got = hop(chain, stage)
         copy.wait()
         total = kept[...].astype(F32) + got[...].astype(F32)
-        if stage < bits - 1:
+        if stage == bits - 1:
+            sums[chain][...] = total
+        else:
             got[...] = total.astype(BF16)
             hop(chain, stage + 1)[0].start()
-        elif not direct:
-            sums[chain][...] = total
-        elif chain == 1:
-            no_ref[...] = DECAY * mo_ref[...] + scale * total
+
+    def weight_grad(chain):
+        order = orders[chain]
+        if direct:
+            pieces = [
+                (start + j, PAIR) for start, size in columns[chain] for j in range(0, size, PAIR)
+            ]
+            for x in range(0, len(pieces), 2):
+                some = pieces[x : x + 2]
+                if chain == 1:
+                    right = [og_ref[:, lo : lo + size] for lo, size in some]
+                    part = dot_nn(mixed_t[...], jnp.concatenate(right, axis=1))
+                else:
+                    right = [hgrad_t[lo : lo + size, :] for lo, size in some]
+                    part = dot_nt(tok_t[...], jnp.concatenate(right, axis=0))
+                part = part.astype(BF16)
+                cols = slice(x * PAIR, x * PAIR + part.shape[1])
+                for slot in range(n):
+                    d = slot_device(slot, n, order)
+                    sources[chain][slot * per : (slot + 1) * per, cols] = part[d * per : (d + 1) * per]
         else:
-            at = 0
-            for start, size in columns[chain]:
-                cols = slice(start, start + size)
-                ni_ref[:, cols] = DECAY * mi_ref[:, cols] + scale * total[:, at : at + size]
-                at += size
-
-    def weight_grad(chain):
-        order = chain_bits(bits, chain % 2 == 1)
-        if direct:
-            at = 0
-            for start, size in columns[chain] or [(0, width)]:
-                for j in range(0, size, QB):
-                    lo = start + j
-                    if chain == 1:
-                        part = dot_nn(mixed_t[...], og_ref[:, lo : lo + QB])
-                    else:
-                        part = dot_nt(tok_t[...], hgrad_t[lo : lo + QB, :])
-                    part = part.astype(BF16)
-                    for slot in range(n):
-                        d = slot_device(slot, n, order)
-                        sources[chain][slot * per : (slot + 1) * per, at : at + QB] = part[
-                            d * per : (d + 1) * per
-                        ]
-                    at += QB
-        else:
-            base, size = (columns[chain] or [(0, width)])[0]
+            base, size = columns[chain][0]
             thin = size // fold
             step = QB if thin % QB == 0 else thin
             strip = 128
@@ -427,14 +437,16 @@
             g = p * two + h
             t = tiles.index((qc, kc))
             hr_ = slice(h * head, (h + 1) * head)
-            ds = u.astype(BF16) * slopes[g, t]
+            a = attn[g, t]
+            wb = slopes[g, t]
+            ds = u.astype(BF16) * (wb + a * (2.0 - wb))
             dq = dot_nn(k_t[g, :, span(kc)], ds)
             if kc == 0:
                 acc[h, :, span(qc)] = dq
             else:
                 acc[h, :, span(qc)] += dq
             one = dot_nt(q_t[p, hr_, span(qc)], ds)
-            two_ = dot_nt(dout_t[p, hr_, span(qc)], attn[g, t])
+            two_ = dot_nt(dout_t[p, hr_, span(qc)], a)
             dk = one if qc == kc else dk + one
             dv = two_ if qc == kc else dv + two_
             if qc == nq - 1:
@@ -455,7 +467,7 @@
 
         if direct:
 
-            @pl.when(p == pairs // 2 - 1)
+            @pl.when(p == pairs - 3)
             def _():
                 weight_grad(2)
 
@@ -463,13 +475,16 @@
         def _():
             advance(0, 1)
             advance(1, 1)
+            if direct:
+                advance(2, 0)
+                weight_grad(3)
 
         @pl.when(p == pairs - 1)
         def _():
-            if direct:
-                advance(2, 0)
             advance(0, 2)
             advance(1, 2)
+            if direct:
+                advance(3, 0)
 
         return carry
 
@@ -484,37 +499,100 @@
 
     lax.fori_loop(0, nq, tokens_back, 0)
 
-    for k in range(nq):
+    if direct:
+        advance(2, 1)
+        advance(0, 3)
+        advance(1, 3)
+    def fill_back(k):
         at = back.chunk(k)
         r = pl.ds(pl.multiple_of(at * QB, QB), QB)
         part = dot_nt(place[r, :], dmix_t[...]).astype(BF16)
         outbox[pl.ds(at * group, group)] = part.reshape(group, cap, width)
-        back.start(k)
-    if not direct:
-        weight_grad(2)
-    weight_grad(3)
-    inbox2[me] = outbox[me]
-    gather_matrix(home_ref, pick)
-    if not direct:
-        advance(2, 0)
-    for stage in range(bits):
-        if stage >= 3:
-            advance(0, stage)
-            advance(1, stage)
-        if stage >= 1:
-            advance(2, stage)
-        advance(3, stage)
-    for k in range(nq):
-        back.finish(k)
+
+    def collect(k):
+        back.arrived(k)
         at = back.chunk(k)
         box = inbox2[pl.ds(at * group, group)].reshape(QB, width)
         part = dot_nn(pick[:, pl.ds(pl.multiple_of(at * QB, QB), QB)], box).astype(BF16)
         if k == 0:
             tok[...] = part
-        elif k < nq - 1:
+        else:
             tok[...] += part
+
+    plan = PLAN if direct else WHOLE_PLAN
+    for what, *args in plan:
+        if what == "fill":
+            fill_back(*args)
+        elif what == "start":
+            back.start(*args)
+        elif what == "sent":
+            back.sent(*args)
+        elif what == "msg":
+            back.copy(*args).start()
+        elif what == "gone":
+            back.copy(*args).wait_send()
+        elif what == "get":
+            collect(*args)
+        elif what == "own":
+            inbox2[me] = outbox[me]
+        elif what == "grad":
+            weight_grad(*args)
+        elif what == "pick":
+            gather_matrix(home_ref, pick)
         else:
-            out_ev[...] = tok[...] + part
+            advance(*args)
+    inbox2[me] = outbox[me]
+    store = pltpu.make_async_copy(tok, out_ev, lsem.at[0])
+    store.start()
+    store.wait()
+
+
+def chain_columns(width, direct):
+    half = width // 2
+    if not direct:
+        return [[(0, width)], [(0, width)], [(width, 3 * half)], [(width + 3 * half, 3 * half)]]
+    parts = ((0, half), (half, PAIR), (half + PAIR, PAIR))
+    late = [[(width * g + at, size) for g in (1, 2, 3)] for at, size in parts]
+    return [[(0, width)], [(0, width)], *late]
+
+
+def finish_kernel(scale, columns, count, *refs):
+    wide, spots, scratch = refs[: count + 3], refs[count + 3 : count + 6], refs[count + 6 :]
+    ev_hbm, *small = wide
+    held, *near, ni_ref, no_ref, isem, osem, psem = scratch
+    loads, stores = [], []
+    parts = osem.shape[0] - 2
+    size = held.shape[0] // parts
+    for i in range(parts):
+        r = pl.ds(i * size, size)
+        loads.append(pltpu.make_async_copy(ev_hbm.at[r], held.at[r], isem.at[i]))
+        stores.append(pltpu.make_async_copy(held.at[r], spots[0].at[r], osem.at[i]))
+    other = [
+        pltpu.make_async_copy(src, dst, psem.at[i]) for i, (src, dst) in enumerate(zip(small, near))
+    ]
+    for load in [*other, *loads]:
+        load.start()
+    for load in other:
+        load.wait()
+    *sums, mi_ref, mo_ref = near
+    no_ref[...] = DECAY * mo_ref[...] + scale * sums[1][...]
+    for chain in range(count):
+        if chain == 1:
+            continue
+        at = 0
+        for start, span in columns[chain]:
+            cols = slice(start, start + span)
+            ni_ref[:, cols] = DECAY * mi_ref[:, cols] + scale * sums[chain][:, at : at + span]
+            at += span
+    stores.append(pltpu.make_async_copy(ni_ref, spots[1], osem.at[parts]))
+    stores.append(pltpu.make_async_copy(no_ref, spots[2], osem.at[parts + 1]))
+    stores[-1].start()
+    stores[-2].start()
+    for load, store in zip(loads, stores):
+        load.wait()
+        store.start()
+    for store in stores:
+        store.wait()
 
 
 def shards(n, events, home_slot, dest_slot, seq_lens, weights, out_grad, momentum_in, momentum_out):
@@ -535,7 +613,8 @@
     sm = pl.BlockSpec(memory_space=pltpu.SMEM)
     hbm = pl.BlockSpec(memory_space=pl.ANY)
     dma = pltpu.SemaphoreType.DMA
-    wides = (width, width, 3 * width // 2, 3 * width // 2)
+    columns = chain_columns(width, direct)
+    wides = [sum(size for _, size in cols) for cols in columns]
     thins = [w // fold for w in wides]
     bufs = [pltpu.VMEM((n * tall, t), BF16) for t in thins]
     for t in thins:
@@ -549,22 +628,16 @@
     ntile = nq * (nq + 1) // 2
     blocks = rows // BLK
     ev_shape = jax.ShapeDtypeStruct(events.shape, BF16)
-    if direct:
-        outs = [
-            ev_shape,
-            jax.ShapeDtypeStruct(momentum_in.shape, F32),
-            jax.ShapeDtypeStruct(momentum_out.shape, F32),
-        ]
-        more = (momentum_in, momentum_out)
-    else:
-        outs = [ev_shape] + [jax.ShapeDtypeStruct((tall, t), F32) for t in thins]
-        more = ()
-    got = pl.pallas_call(
-        functools.partial(step_kernel, n, scale, direct),
-        out_shape=outs,
-        in_specs=[sm, vm, vm, vm, hbm, hbm] + [vm] * len(more),
-        out_specs=[vm] * len(outs),
+    ev, *parts = pl.pallas_call(
+        functools.partial(step_kernel, n, direct),
+        out_shape=[ev_shape] + [jax.ShapeDtypeStruct((tall, t), F32) for t in thins],
+        in_specs=[hbm] * 6,
+        out_specs=[hbm] + [vm] * len(thins),
         scratch_shapes=[
+            pltpu.SMEM(seq_lens.shape, jnp.int32),
+            area(1, rows, kind=jnp.int32),
+            area(1, rows, kind=jnp.int32),
+            area(rows, width),
             area(width, 5 * width),
             area(rows, width),
             area(width, rows),
@@ -591,32 +664,47 @@
             area(pairs, PAIR, rows),
             area(PAIR // head, head, rows, kind=F32),
             area(max(1, blocks * (blocks - 1) // 2), PAIR, QB),
-            dma((2,)),
+            dma((6,)),
             dma((n,)),
             dma((n,)),
             dma((n,)),
             dma((n,)),
-            dma((4 * bits,)),
-            dma((4 * bits,)),
+            dma((len(thins) * bits,)),
+            dma((len(thins) * bits,)),
         ]
         + bufs,
         compiler_params=pltpu.CompilerParams(
             collective_id=0, has_side_effects=True, vmem_limit_bytes=VMEM_LIMIT
         ),
         name="step",
-    )(seq_lens, home, dest, events, weights, out_grad, *more)
-    if direct:
-        return tuple(got)
-    ev, *parts = got
-    f0, f1, f2, f3 = [
-        f.reshape(fold, per, f.shape[1]).transpose(1, 0, 2).reshape(per, fold * f.shape[1])
-        for f in parts
-    ]
-    return (
-        ev,
-        DECAY * momentum_in + scale * jnp.concatenate([f0, f2, f3], axis=1),
-        DECAY * momentum_out + scale * f1,
-    )
+    )(seq_lens, home, dest, events, weights, out_grad)
+    if not direct:
+        parts = [
+            f.reshape(fold, per, f.shape[1]).transpose(1, 0, 2).reshape(per, fold * f.shape[1])
+            for f in parts
+        ]
+    small = (*parts, momentum_in, momentum_out)
+    return pl.pallas_call(
+        functools.partial(finish_kernel, scale, columns, len(parts)),
+        out_shape=[
+            ev_shape,
+            jax.ShapeDtypeStruct(momentum_in.shape, F32),
+            jax.ShapeDtypeStruct(momentum_out.shape, F32),
+        ],
+        in_specs=[hbm] * (len(small) + 1),
+        out_specs=[hbm] * 3,
+        scratch_shapes=[
+            area(rows, width),
+            *(area(*x.shape, kind=F32) for x in small),
+            area(*momentum_in.shape, kind=F32),
+            area(*momentum_out.shape, kind=F32),
+            dma((4,)),
+            dma((6,)),
+            dma((len(small),)),
+        ],
+        compiler_params=pltpu.CompilerParams(vmem_limit_bytes=VMEM_LIMIT),
+        name="finish",
+    )(ev, *small)
 
 
 def solution(mesh):

time: 105 us -> 100 us (0.952)
  local copies, waits for them, and re-layouts: 5.2 us -> 0 us
    unnamed x3 -> x0, local copies, waits for them, and re-layouts: 5.2 us -> none
    pallas_call x1 -> x2, Pallas kernels: 99.2 us -> 99 us  [the longest x1 96.7 us: shards(): pl.pallas_call(functools.partial(step_kernel, n, direct), out_shape=[ev_s...]
where the time goes in v2:
time: 100 us; the launch traced here: 99.8 us
  Pallas kernels  99 us (99%)
    pallas_call x1, Pallas kernels, shards(): pl.pallas_call(functools.partial(step_kernel, n, direct), out_shape=[ev_s...  96.7 us
    pallas_call x1, Pallas kernels, shards(): pl.pallas_call(functools.partial(finish_kernel, scale, columns, len(parts...  2.35 us

profile of v2, /device:TPU:0, one launch (start us, length us, event | category | flops | bytes accessed | tf_op | source)
XLA Modules:
  0.0 99.8 jit_solution(5767432722009899735)
XLA Ops:
  0.6 96.7 %step.1 = (bf16[1024,512]{1,0:T(8,128)(2,1)}, f32[16,512]{1,0:T(8,128)}, f32[16,512]{1,0:T(8,128)}, f32[16,768]{1,0:T(8,128)}, f32[16,384]{1,0:T(8,128)}, /*index=5*/f32[16,384]{1,0:T(8,128)}) custom-call(s32[2]{0:T(128)} %lens_hbm.1, s32[1,1024]{1,0:T(1,128)} %bitcast.2, s32[1,1024]{1,0:T(1,128)} %bitcast.3, bf16[1024,512]{1,0:T(8,128)(2,1)} %ev_hbm.1, ...), custom_call_target="tpu_custom_call" | custom-call | tf_op jit(solution)/shard_map/step/pallas_call | solution.py:631
  97.3 2.4 %finish.1 = (bf16[1024,512]{1,0:T(8,128)(2,1)}, f32[16,2048]{1,0:T(8,128)}, f32[16,512]{1,0:T(8,128)}) custom-call(bf16[1024,512]{1,0:T(8,128)(2,1)} %get-tuple-element.9.refs_0_, f32[16,512]{1,0:T(8,128)} %get-tuple-element.10.refs_1_, f32[16,512]{1,0:T(8,128)} %get-tuple-element.11.refs_2_, f32[16,768]{1,0:T(8,128)} %get-tuple-element.12.refs_3_, ...), custom_call_target="tpu_custom_call" | custom-call | tf_op jit(solution)/shard_map/finish/pallas_call | solution.py:687

commit v3 on v2

--- a/solution.py
+++ b/solution.py
@@ -17,9 +17,11 @@
 F32 = jnp.float32
 BF16 = jnp.bfloat16
 VMEM_LIMIT = 67 * 1000 * 1000
-LAG = 2
+LAG = 4
+BACK_LAG = 2
+DEEP = 1
 LATE = ((4, 0), (3, 1), (2, 2), (4, 1), (0, 4), (1, 4), (3, 2), (2, 3), (4, 2), (3, 3), (2, 4), (4, 3), (3, 4), (4, 4))
-PLAN = (('fill', 3), ('fill', 1), ('msg', 3, 0), ('msg', 1, 0), ('msg', 3, 1), ('msg', 1, 1), ('msg', 3, 2), ('msg', 1, 2), ('msg', 3, 3), ('msg', 1, 3), ('fill', 2), ('fill', 0), ('own',), ('msg', 3, 4), ('msg', 1, 4), ('msg', 3, 5), ('msg', 1, 5), ('grad', 4), ('gone', 3, 0), ('gone', 1, 0), ('msg', 3, 6), ('msg', 1, 6), ('add', 3, 1), ('add', 2, 2), ('gone', 3, 1), ('gone', 1, 1), ('msg', 3, 7), ('msg', 1, 7), ('add', 4, 0), ('gone', 3, 2), ('gone', 1, 2), ('msg', 2, 0), ('msg', 0, 1), ('add', 0, 4), ('add', 1, 4), ('gone', 3, 3), ('gone', 1, 3), ('msg', 2, 1), ('msg', 0, 2), ('add', 4, 1), ('add', 3, 2), ('gone', 3, 4), ('gone', 1, 4), ('msg', 2, 2), ('msg', 0, 3), ('add', 2, 3), ('gone', 3, 5), ('gone', 1, 5), ('msg', 2, 3), ('msg', 0, 4), ('add', 4, 2), ('add', 3, 3), ('gone', 3, 6), ('gone', 1, 6), ('msg', 2, 4), ('msg', 0, 5), ('gone', 3, 7), ('gone', 1, 7), ('msg', 2, 5), ('msg', 0, 6), ('add', 2, 4), ('add', 4, 3), ('add', 3, 4), ('gone', 2, 0), ('gone', 0, 1), ('msg', 2, 6), ('msg', 0, 7), ('gone', 2, 1), ('gone', 0, 2), ('msg', 2, 7), ('add', 4, 4), ('pick',), ('get', 0), ('get', 1), ('get', 2), ('get', 3), ('gone', 2, 2), ('gone', 0, 3), ('gone', 2, 3), ('gone', 0, 4), ('gone', 2, 4), ('gone', 0, 5), ('gone', 2, 5), ('gone', 0, 6), ('gone', 2, 6), ('gone', 0, 7), ('gone', 2, 7))
+PLAN = (('fill', 3), ('fill', 1), ('msg', 3, 0), ('msg', 1, 0), ('msg', 3, 1), ('msg', 1, 1), ('msg', 3, 2), ('msg', 1, 2), ('msg', 3, 3), ('msg', 1, 3), ('fill', 0), ('fill', 2), ('own',), ('msg', 3, 4), ('msg', 1, 4), ('msg', 3, 5), ('msg', 1, 5), ('grad', 4), ('gone', 3, 0), ('gone', 1, 0), ('msg', 3, 6), ('msg', 1, 6), ('add', 2, 1), ('add', 3, 1), ('gone', 3, 1), ('gone', 1, 1), ('msg', 3, 7), ('msg', 1, 7), ('add', 4, 0), ('gone', 3, 2), ('gone', 1, 2), ('msg', 2, 0), ('msg', 0, 1), ('add', 0, 4), ('add', 1, 4), ('gone', 3, 3), ('gone', 1, 3), ('msg', 2, 1), ('msg', 0, 2), ('pick',), ('add', 2, 2), ('add', 4, 1), ('add', 3, 2), ('gone', 3, 4), ('gone', 1, 4), ('msg', 2, 2), ('msg', 0, 3), ('add', 2, 3), ('gone', 3, 5), ('gone', 1, 5), ('msg', 2, 3), ('msg', 0, 4), ('add', 4, 2), ('add', 3, 3), ('gone', 3, 6), ('gone', 1, 6), ('msg', 2, 4), ('msg', 0, 5), ('gone', 3, 7), ('gone', 1, 7), ('msg', 2, 5), ('msg', 0, 6), ('get', 1, True), ('add', 2, 4), ('add', 4, 3), ('add', 3, 4), ('gone', 2, 0), ('gone', 0, 1), ('msg', 2, 6), ('msg', 0, 7), ('gone', 2, 1), ('gone', 0, 2), ('msg', 2, 7), ('get', 0), ('get', 3), ('add', 4, 4), ('get', 2, False, True), ('gone', 2, 2), ('gone', 0, 3), ('gone', 2, 3), ('gone', 0, 4), ('gone', 2, 4), ('gone', 0, 5), ('gone', 2, 5), ('gone', 0, 6), ('gone', 2, 6), ('gone', 0, 7), ('gone', 2, 7))
 WHOLE_PLAN = (
     *((what, k) for k in range(4) for what in ("fill", "start")),
     ("grad", 2),
@@ -28,7 +30,10 @@
     *(("add", chain, stage) for stage in (3, 4, 5, 6) for chain in (0, 1)),
     *(("add", chain, stage) for stage in range(7) for chain in (2, 3)),
     ("own",),
-    *(("get", k) for k in range(4)),
+    ("get", 0, True),
+    ("get", 1),
+    ("get", 2),
+    ("get", 3, False, True),
     *(("sent", k) for k in range(4)),
 )
 
@@ -424,31 +429,35 @@
     def backward(p, carry):
         work = [(h, qc, kc) for h in range(two) for kc in range(nq) for qc in range(kc, nq)]
         held = {}
+        ready = {}
         dk = dv = None
-        for i in range(len(work) + LAG):
+        for i in range(len(work) + BACK_LAG + DEEP):
             if i < len(work):
                 h, qc, kc = work[i]
                 d = linked(dout_t[p, :, span(qc)], qc, kc)
                 held[i] = dot_nn(v_z[p * two + h, span(kc), :], d)
-            if i < LAG:
+            j = i - BACK_LAG
+            if 0 <= j < len(work):
+                h, qc, kc = work[j]
+                a = attn[p * two + h, tiles.index((qc, kc))]
+                wb = slopes[p * two + h, tiles.index((qc, kc))]
+                ready[j] = held.pop(j).astype(BF16) * (wb + a * (2.0 - wb))
+            j = i - BACK_LAG - DEEP
+            if j < 0:
                 continue
-            h, qc, kc = work[i - LAG]
-            u = held.pop(i - LAG)
+            h, qc, kc = work[j]
+            ds = ready.pop(j)
             g = p * two + h
-            t = tiles.index((qc, kc))
-            hr_ = slice(h * head, (h + 1) * head)
-            a = attn[g, t]
-            wb = slopes[g, t]
-            ds = u.astype(BF16) * (wb + a * (2.0 - wb))
+            mine = slice(h * head, (h + 1) * head)
             dq = dot_nn(k_t[g, :, span(kc)], ds)
             if kc == 0:
                 acc[h, :, span(qc)] = dq
             else:
                 acc[h, :, span(qc)] += dq
-            one = dot_nt(q_t[p, hr_, span(qc)], ds)
-            two_ = dot_nt(dout_t[p, hr_, span(qc)], a)
-            dk = one if qc == kc else dk + one
-            dv = two_ if qc == kc else dv + two_
+            more_k = dot_nt(q_t[p, mine, span(qc)], ds)
+            more_v = dot_nt(dout_t[p, mine, span(qc)], attn[g, tiles.index((qc, kc))])
+            dk = more_k if qc == kc else dk + more_k
+            dv = more_v if qc == kc else dv + more_v
             if qc == nq - 1:
                 for grp, val in ((1, dv), (3, dk)):
                     rs = pl.ds(pl.multiple_of(grp * width + p * PAIR + h * head, head), head)
@@ -470,21 +479,27 @@
             @pl.when(p == pairs - 3)
             def _():
                 weight_grad(2)
+                advance(0, 1)
+                advance(1, 1)
 
         @pl.when(p == pairs - 2)
         def _():
-            advance(0, 1)
-            advance(1, 1)
             if direct:
                 advance(2, 0)
                 weight_grad(3)
+                advance(0, 2)
+                advance(1, 2)
 
         @pl.when(p == pairs - 1)
         def _():
-            advance(0, 2)
-            advance(1, 2)
             if direct:
                 advance(3, 0)
+                advance(0, 3)
+                advance(1, 3)
+            else:
+                for stage in (1, 2):
+                    advance(0, stage)
+                    advance(1, stage)
 
         return carry
 
@@ -500,24 +515,30 @@
     lax.fori_loop(0, nq, tokens_back, 0)
 
     if direct:
-        advance(2, 1)
-        advance(0, 3)
-        advance(1, 3)
+        pass
     def fill_back(k):
         at = back.chunk(k)
         r = pl.ds(pl.multiple_of(at * QB, QB), QB)
         part = dot_nt(place[r, :], dmix_t[...]).astype(BF16)
         outbox[pl.ds(at * group, group)] = part.reshape(group, cap, width)
 
-    def collect(k):
+    stores = []
+
+    def collect(k, first=False, last=False):
         back.arrived(k)
         at = back.chunk(k)
         box = inbox2[pl.ds(at * group, group)].reshape(QB, width)
-        part = dot_nn(pick[:, pl.ds(pl.multiple_of(at * QB, QB), QB)], box).astype(BF16)
-        if k == 0:
-            tok[...] = part
-        else:
-            tok[...] += part
+        cols = pl.ds(pl.multiple_of(at * QB, QB), QB)
+        if not last:
+            part = dot_nn(pick[:, cols], box).astype(BF16)
+            tok[...] = part if first else tok[...] + part
+            return
+        for c in range(nq):
+            tok[span(c), :] += dot_nn(pick[span(c), cols], box).astype(BF16)
+            stores.append(
+                pltpu.make_async_copy(tok.at[span(c)], out_ev.at[span(c)], lsem.at[c])
+            )
+            stores[-1].start()
 
     plan = PLAN if direct else WHOLE_PLAN
     for what, *args in plan:
@@ -542,9 +563,8 @@
         else:
             advance(*args)
     inbox2[me] = outbox[me]
-    store = pltpu.make_async_copy(tok, out_ev, lsem.at[0])
-    store.start()
-    store.wait()
+    for store in stores:
+        store.wait()
 
 
 def chain_columns(width, direct):

time: 100 us -> 98.4 us (0.984)
  Pallas kernels: 99 us -> 97.2 us
    pallas_call x1, Pallas kernels: 96.7 us -> 94.8 us  [shards(): pl.pallas_call(functools.partial(step_kernel, n, direct), out_shape=[ev_s...]
where the time goes in v3:
time: 98.4 us; the launch traced here: 98 us
  Pallas kernels  97.2 us (99%)
    pallas_call x1, Pallas kernels, shards(): pl.pallas_call(functools.partial(step_kernel, n, direct), out_shape=[ev_s...  94.8 us
    pallas_call x1, Pallas kernels, shards(): pl.pallas_call(functools.partial(finish_kernel, scale, columns, len(parts...  2.35 us

profile of v3, /device:TPU:0, one launch (start us, length us, event | category | flops | bytes accessed | tf_op | source)
XLA Modules:
  0.0 98.0 jit_solution(13189154597269122554)
XLA Ops:
  0.6 94.8 %step.1 = (bf16[1024,512]{1,0:T(8,128)(2,1)}, f32[16,512]{1,0:T(8,128)}, f32[16,512]{1,0:T(8,128)}, f32[16,768]{1,0:T(8,128)}, f32[16,384]{1,0:T(8,128)}, /*index=5*/f32[16,384]{1,0:T(8,128)}) custom-call(s32[2]{0:T(128)} %lens_hbm.1, s32[1,1024]{1,0:T(1,128)} %bitcast.2, s32[1,1024]{1,0:T(1,128)} %bitcast.3, bf16[1024,512]{1,0:T(8,128)(2,1)} %ev_hbm.1, ...), custom_call_target="tpu_custom_call" | custom-call | tf_op jit(solution)/shard_map/step/pallas_call | solution.py:651
  95.4 2.4 %finish.1 = (bf16[1024,512]{1,0:T(8,128)(2,1)}, f32[16,2048]{1,0:T(8,128)}, f32[16,512]{1,0:T(8,128)}) custom-call(bf16[1024,512]{1,0:T(8,128)(2,1)} %get-tuple-element.9.refs_0_, f32[16,512]{1,0:T(8,128)} %get-tuple-element.10.refs_1_, f32[16,512]{1,0:T(8,128)} %get-tuple-element.11.refs_2_, f32[16,768]{1,0:T(8,128)} %get-tuple-element.12.refs_3_, ...), custom_call_target="tpu_custom_call" | custom-call | tf_op jit(solution)/shard_map/finish/pallas_call | solution.py:707

commit v4 on v3

--- a/solution.py
+++ b/solution.py
@@ -205,8 +205,8 @@
         at = there.chunk(k)
         part = dot_nn(scatter_chunk(home_ref, at * QB, QB), ev_ref[...]).astype(BF16)
         outbox[pl.ds(at * group, group)] = part.reshape(group, cap, width)
-        if k == 0:
-            pl.semaphore_wait(barrier, n - 1)
+    pl.semaphore_wait(barrier, n - 1)
+    for k in (*range(nq // 2, nq), *range(nq // 2 - 1, -1, -1)):
         there.start(k)
     inbox[me] = outbox[me]
     for load in loads[2:]:

time: 98.4 us -> 97.3 us (0.989)
  Pallas kernels: 97.2 us -> 96 us
    pallas_call x1, Pallas kernels: 94.8 us -> 93.7 us  [shards(): pl.pallas_call(functools.partial(step_kernel, n, direct), out_shape=[ev_s...]
where the time goes in v4:
time: 97.3 us; the launch traced here: 96.8 us
  Pallas kernels  96 us (99%)
    pallas_call x1, Pallas kernels, shards(): pl.pallas_call(functools.partial(step_kernel, n, direct), out_shape=[ev_s...  93.7 us
    pallas_call x1, Pallas kernels, shards(): pl.pallas_call(functools.partial(finish_kernel, scale, columns, len(parts...  2.35 us

profile of v4, /device:TPU:0, one launch (start us, length us, event | category | flops | bytes accessed | tf_op | source)
XLA Modules:
  0.0 96.8 jit_solution(5322175306004560800)
XLA Ops:
  0.6 93.7 %step.1 = (bf16[1024,512]{1,0:T(8,128)(2,1)}, f32[16,512]{1,0:T(8,128)}, f32[16,512]{1,0:T(8,128)}, f32[16,768]{1,0:T(8,128)}, f32[16,384]{1,0:T(8,128)}, /*index=5*/f32[16,384]{1,0:T(8,128)}) custom-call(s32[2]{0:T(128)} %lens_hbm.1, s32[1,1024]{1,0:T(1,128)} %bitcast.2, s32[1,1024]{1,0:T(1,128)} %bitcast.3, bf16[1024,512]{1,0:T(8,128)(2,1)} %ev_hbm.1, ...), custom_call_target="tpu_custom_call" | custom-call | tf_op jit(solution)/shard_map/step/pallas_call | solution.py:651
  94.3 2.4 %finish.1 = (bf16[1024,512]{1,0:T(8,128)(2,1)}, f32[16,2048]{1,0:T(8,128)}, f32[16,512]{1,0:T(8,128)}) custom-call(bf16[1024,512]{1,0:T(8,128)(2,1)} %get-tuple-element.9.refs_0_, f32[16,512]{1,0:T(8,128)} %get-tuple-element.10.refs_1_, f32[16,512]{1,0:T(8,128)} %get-tuple-element.11.refs_2_, f32[16,768]{1,0:T(8,128)} %get-tuple-element.12.refs_3_, ...), custom_call_target="tpu_custom_call" | custom-call | tf_op jit(solution)/shard_map/finish/pallas_call | solution.py:707

commit v5 on v4

--- a/solution.py
+++ b/solution.py
@@ -239,12 +239,13 @@
         i, j = qc * QB // BLK, kc * QB // BLK
         return value if i == j else value * cross[links.index((i, j))]
 
-    for k in range(nq):
+    arrivals = (*range(nq // 2 - 1, -1, -1), *range(nq // 2, nq))
+    for k in arrivals:
         there.finish(k)
         at = there.chunk(k)
         box = inbox[pl.ds(at * group, group)].reshape(QB, width)
         part = dot_nn(pick[:, pl.ds(pl.multiple_of(at * QB, QB), QB)], box).astype(BF16)
-        if k == 0:
+        if k == arrivals[0]:
             tok[...] = part
         else:
             tok[...] += part

time: 97.3 us -> 97.3 us (level)
  no operation moved by 1% of the time
where the time goes in v5:
time: 97.3 us; the launch traced here: 96.8 us
  Pallas kernels  96 us (99%)
    pallas_call x1, Pallas kernels, shards(): pl.pallas_call(functools.partial(step_kernel, n, direct), out_shape=[ev_s...  93.7 us
    pallas_call x1, Pallas kernels, shards(): pl.pallas_call(functools.partial(finish_kernel, scale, columns, len(parts...  2.35 us

profile of v5, /device:TPU:0, one launch (start us, length us, event | category | flops | bytes accessed | tf_op | source)
XLA Modules:
  0.0 96.8 jit_solution(6101866551700045353)
XLA Ops:
  0.6 93.7 %step.1 = (bf16[1024,512]{1,0:T(8,128)(2,1)}, f32[16,512]{1,0:T(8,128)}, f32[16,512]{1,0:T(8,128)}, f32[16,768]{1,0:T(8,128)}, f32[16,384]{1,0:T(8,128)}, /*index=5*/f32[16,384]{1,0:T(8,128)}) custom-call(s32[2]{0:T(128)} %lens_hbm.1, s32[1,1024]{1,0:T(1,128)} %bitcast.2, s32[1,1024]{1,0:T(1,128)} %bitcast.3, bf16[1024,512]{1,0:T(8,128)(2,1)} %ev_hbm.1, ...), custom_call_target="tpu_custom_call" | custom-call | tf_op jit(solution)/shard_map/step/pallas_call | solution.py:652
  94.3 2.4 %finish.1 = (bf16[1024,512]{1,0:T(8,128)(2,1)}, f32[16,2048]{1,0:T(8,128)}, f32[16,512]{1,0:T(8,128)}) custom-call(bf16[1024,512]{1,0:T(8,128)(2,1)} %get-tuple-element.9.refs_0_, f32[16,512]{1,0:T(8,128)} %get-tuple-element.10.refs_1_, f32[16,512]{1,0:T(8,128)} %get-tuple-element.11.refs_2_, f32[16,768]{1,0:T(8,128)} %get-tuple-element.12.refs_3_, ...), custom_call_target="tpu_custom_call" | custom-call | tf_op jit(solution)/shard_map/finish/pallas_call | solution.py:708
